TPU v7x, 512 devices: a whole 4x8x8 slice. The times are simulated.
512 devices in a mesh: section: 2 (over core), sy: 8 (over y), sx: 8 (over z), mb: 4 (over x).
Axes of the slice: x: 4, y: 8, z: 8, core: 2. Of those that a mesh axis runs over, the one named last changes fastest.
Arguments:
- frames: bfloat16 [4, 512, 512, 128], P('mb', 'sy', 'sx'), may hold values from -6 to 6
- encode_weight: bfloat16 [512, 384], replicated, may hold values from -0.25 to 0.25
- conv_weight: bfloat16 [2, 1, 3456, 384], P('section', None, ('sy', 'sx')), may hold values from -0.109375 to 0.109375
- norm_gain: float32 [2, 1, 384], P('section'), may hold values from 0.1 to 1.9
- head_weight: bfloat16 [384, 256], replicated, may hold values from -0.3125 to 0.3125
- prior_logits: bfloat16 [4, 256, 256, 256], P('mb', 'sy', 'sx'), may hold values from -12 to 249
- target_bins: int32 [4, 256, 256], P('mb', 'sy', 'sx'), may hold values from 0 to 255
Outputs:
- section_features: bfloat16 [2, 4, 256, 256, 384], P('section', 'mb', 'sy', 'sx')
- head_step: float32 [384, 256], P('section')
- mean_loss: float32 [], replicated
All inputs are finite; a program needn't handle non-finite values.
Results may differ from a plain program's by a relative error of at most 0.008.
Values may be sent and summed in bfloat16 or wider, within the bound.
No kernel may reach another device: no remote copies, remote signals or barrier semaphores. Data moves between devices by JAX's collectives and lax.ppermute only.
A program may use at most 64 MiB of HBM per device.

v0:
```python
import jax
import jax.numpy as jnp
from jax import lax
from jax.sharding import PartitionSpec as P

FIRST_DILATION = 1


def padded_2(block, sides, width):
    for axis, dim in sides:
        count = lax.axis_size(axis)
        forward = [(i, i + 1) for i in range(count - 1)]
        backward = [(target, source) for source, target in forward]
        low = lax.ppermute(
            lax.slice_in_dim(block, block.shape[dim] - width, None, axis=dim), axis, forward
        )
        high = lax.ppermute(lax.slice_in_dim(block, 0, width, axis=dim), axis, backward)
        block = jnp.concatenate([low, block, high], axis=dim)
    return block


def from_behind(block, axis, distance):
    devices = range(lax.axis_size(axis))
    route = [(i - distance, i) for i in devices if i - distance in devices]
    return lax.ppermute(block, axis, route)


def norm_gelu(activations, gain):
    values = activations.astype(jnp.float32)
    center = jnp.mean(values, axis=-1, keepdims=True)
    offset = values - center
    spread = jnp.mean(offset * offset, axis=-1, keepdims=True)
    normed = offset * lax.rsqrt(spread + 1e-05) * gain
    return jax.nn.gelu(normed, approximate=False).astype(jnp.bfloat16)


def per_device(
    frames, encode_weight, conv_weight, norm_gain, head_weight, prior_logits, target_bins
):
    first_section = lax.axis_index("section") == 0
    micro_count = frames.shape[0]
    side_cells = frames.shape[1] // 2
    input_width = frames.shape[3]
    channels = encode_weight.shape[1]
    bins_count = head_weight.shape[1]
    parts_y = lax.axis_size("sy")
    parts_x = lax.axis_size("sx")
    cell_count = side_cells * side_cells
    kernel = encode_weight.reshape(2, 2, input_width, channels)
    grad_total = jnp.zeros((channels, bins_count), jnp.float32)
    loss_total = jnp.zeros((), jnp.float32)
    first_out = []
    second_out = []
    handed = None
    for tick_index in range(micro_count + 1):
        if tick_index == 0:
            blocks = frames[0].reshape(side_cells, 2, side_cells, 2, input_width)
            activations = jnp.einsum(
                "apbqc,pqco->abo", blocks, kernel, preferred_element_type=jnp.float32
            ).astype(jnp.bfloat16)
        else:
            activations = handed
        apply_reach = FIRST_DILATION * 2**0
        hidden = norm_gelu(activations, norm_gain[0, 0])
        haloed = padded_2(hidden, (("sy", 0), ("sx", 1)), apply_reach)
        zero_padded = jnp.pad(
            hidden, ((apply_reach, apply_reach), (apply_reach, apply_reach), (0, 0))
        )
        apply_padded = jnp.where(first_section, haloed, zero_padded)
        windows = [
            apply_padded[
                tap_row * apply_reach : tap_row * apply_reach + side_cells,
                tap_column * apply_reach : tap_column * apply_reach + side_cells,
            ]
            for tap_row in range(3)
            for tap_column in range(3)
        ]
        patches = jnp.concatenate(windows, axis=2).reshape(cell_count, 9 * channels)
        summed = jnp.dot(
            patches,
            lax.all_gather(conv_weight[0, 0], ("sy", "sx"), axis=0, tiled=True),
            preferred_element_type=jnp.float32,
        )
        activations = (
            activations.astype(jnp.float32) + summed.reshape(side_cells, side_cells, channels)
        ).astype(jnp.bfloat16)
        if tick_index < micro_count:
            first_out.append(activations)
        rows_y = side_cells // parts_y
        rows_x = side_cells // parts_x
        plain_view = activations.reshape(parts_y, rows_y, parts_x, rows_x, channels)
        spaced = activations.reshape(rows_y, parts_y, rows_x, parts_x, channels).transpose(
            1, 0, 3, 2, 4
        )
        outgoing = jnp.where(first_section, spaced, plain_view)
        arrived = lax.all_to_all(
            lax.all_to_all(outgoing, "sy", split_axis=0, concat_axis=0, tiled=True),
            "sx",
            split_axis=2,
            concat_axis=2,
            tiled=True,
        )
        direct = arrived.reshape(side_cells, side_cells, channels)
        restored = arrived.transpose(1, 0, 3, 2, 4).reshape(side_cells, side_cells, channels)
        moved = jnp.where(first_section, direct, restored)
        if tick_index >= 1:
            second_out.append(moved)
            flat_rows = moved.reshape(cell_count, channels)
            logits = jnp.dot(flat_rows, head_weight, preferred_element_type=jnp.float32)
            logits = logits + prior_logits[tick_index - 1].reshape(cell_count, bins_count).astype(
                jnp.float32
            )
            row_top = jnp.max(logits, axis=1, keepdims=True)
            shifted = logits - row_top
            exp_terms = jnp.exp(shifted)
            exp_total = jnp.sum(exp_terms, axis=1, keepdims=True)
            softmax_rows = exp_terms / exp_total
            onehot = (
                target_bins[tick_index - 1].reshape(cell_count, 1)
                == lax.broadcasted_iota(jnp.int32, (1, bins_count), 1)
            ).astype(jnp.float32)
            loss_sum = jnp.sum(jnp.log(exp_total[:, 0]) - jnp.sum(shifted * onehot, axis=1))
            delta_rows = (softmax_rows - onehot).astype(jnp.bfloat16)
            grad_part = lax.dot_general(
                flat_rows, delta_rows, (((0,), (0,)), ((), ())), preferred_element_type=jnp.float32
            )
            grad_part, loss_sum = (grad_part, loss_sum)
            grad_total = jnp.where(first_section, 0.0, grad_part)
            loss_total = jnp.where(first_section, 0.0, loss_sum)
        if tick_index < micro_count:
            handed = from_behind(moved, "section", 1)
    stacked = jnp.stack([jnp.where(first_section, first_out[0], second_out[0])])[None]
    gradient, loss_all = lax.psum((grad_total, loss_total), ("sy", "sx", "mb"))
    head_full = gradient * lax.rsqrt(jnp.mean(gradient * gradient) + 1e-06)
    mean_local = loss_all / (micro_count * lax.axis_size("mb") * cell_count * parts_y * parts_x)
    half_rows = channels // 2
    sent_rows, sent_loss = (
        from_behind(head_full[:half_rows].astype(jnp.bfloat16), "section", -1).astype(jnp.float32),
        from_behind(mean_local.astype(jnp.bfloat16), "section", -1).astype(mean_local.dtype),
    )
    head_step = jnp.where(first_section, sent_rows, head_full[half_rows:])
    mean_loss = jnp.where(first_section, sent_loss, mean_local)
    return (stacked, head_step, mean_loss)


def solution(mesh):
    placed = (
        P("mb", "sy", "sx", None),
        P(),
        P("section", None, ("sy", "sx"), None),
        P("section", None, None),
        P(),
        P("mb", "sy", "sx", None),
        P("mb", "sy", "sx"),
    )
    return jax.shard_map(
        per_device,
        mesh=mesh,
        in_specs=placed,
        out_specs=(P("section", "mb", "sy", "sx", None), P("section", None), P()),
        check_vma=False,
    )
```

profile of v0, /device:TPU:1, one launch (start us, length us, event | category | flops | bytes accessed | tf_op | source)
XLA Modules:
  0.0 957.4 jit_solution(2720262242174057233)
XLA Ops:
  7.2 1.5 copy.50
  9.5 2.0 convert_reduce_fusion.1
  12.0 3.8 fusion.20
  15.9 4.0 collective-permute-start
  21.2 3.3 collective-permute-done.1
  24.6 4.0 collective-permute-start.2
  29.9 4.2 collective-permute-done.3
  45.5 57.8 %all-gather.3.cloned.1.call-done = bf16[1,1,3456,384]{3,1,0,2:T(2,128)(2,1)} async-done(((bf16[1,1,54,384]{3,1,0,2:T(2,128)(2,1)}), bf16[1,1,3456,384]{3,1,0,2:T(2,128)(2,1)}) %all-gather.3.cloned.1.call-update) | async-done | bytes 2654224 | tf_op jit(solution)/shard_map/all_gather | solution.py:81
  103.3 8.4 fusion.22
  112.4 23.7 %all_to_all.20 = bf16[8,4,8,4,384]{4,3,1,2,0:T(4,128)(2,1)S(1)} all-to-all(bf16[8,4,8,4,384]{4,3,1,2,0:T(4,128)(2,1)S(1)} %bitcast_select_fusion.2), channel_id=1, replica_groups=mesh['section'=2,'sy'=8,'sx'=8,'mb'=4] {'sy'}, dimensions={0} | all-to-all | bytes 1572864 | tf_op jit(solution)/shard_map/all_to_all | solution.py:97
  136.3 19.7 %all_to_all.21 = bf16[8,4,8,4,384]{4,3,1,0,2:T(4,128)(2,1)S(1)} all-to-all(bf16[8,4,8,4,384]{4,3,1,0,2:T(4,128)(2,1)S(1)} %copy.53), channel_id=1, replica_groups=mesh['section'=2,'sy'=8,'sx'=8,'mb'=4] {'sx'}, dimensions={2} | all-to-all | bytes 1572864 | tf_op jit(solution)/shard_map/all_to_all | solution.py:96
  157.3 1.5 collective-permute-start.4
  158.8 9.2 collective-permute-done.4
  168.8 3.8 fusion.13
  175.3 3.3 collective-permute-done.6
  178.7 2.2 collective-permute-start.7
  182.2 3.6 collective-permute-done.8
  189.1 3.9 fusion.24
  193.6 24.2 %all_to_all.22 = bf16[8,4,8,4,384]{4,3,1,2,0:T(4,128)(2,1)S(1)} all-to-all(bf16[8,4,8,4,384]{4,3,1,2,0:T(4,128)(2,1)S(1)} %bitcast_select_fusion.1), channel_id=1, replica_groups=mesh['section'=2,'sy'=8,'sx'=8,'mb'=4] {'sy'}, dimensions={0} | all-to-all | bytes 1572864 | tf_op jit(solution)/shard_map/all_to_all | solution.py:97
  219.0 3.5 all-to-all-start.3
  225.1 16.5 %all-to-all-done.3 = bf16[8,4,8,4,384]{4,3,1,0,2:T(4,128)(2,1)S(1)} async-done(((bf16[8,4,8,4,384]{4,3,1,0,2:T(4,128)(2,1)}), bf16[8,4,8,4,384]{4,3,1,0,2:T(4,128)(2,1)S(1)}, u32[]{:S(2)}, u32[]{:S(2)}) %all-to-all-start.3) | async-done | bytes 786464 | tf_op jit(solution)/shard_map/all_to_all | solution.py:96
  248.7 575.3 %psum.15 = f32[]{:T(128)} all-reduce(f32[]{:T(128)S(6)} %select_n.85), channel_id=1, replica_groups=mesh['section'=2,'sy'=8,'sx'=8,'mb'=4] {'sy','sx','mb'}, use_global_device_ids=true, to_apply=%region_10.11 | all-reduce | flops 1 | bytes 8 | tf_op jit(solution)/shard_map/psum | solution.py:133
  824.8 117.5 %collective-permute-start.10 = (bf16[]{:T(256)}, bf16[]{:T(256)}, u32[]{:S(2)}, u32[]{:S(2)}) collective-permute-start(bf16[]{:T(256)} %convert_element_type.60), channel_id=1, source_target_pairs={{256,0},{257,1},{258,2},{259,3},{260,4},{261,5},{262,6},{263,7},{2... | collective-permute-start | bytes 14 | tf_op jit(solution)/shard_map/ppermute | solution.py:25
  942.3 1.7 multiply_reduce_fusion
  (90 shorter events, 40.6 us)
Async XLA Ops:
  7.2 2.3 copy-start
  7.2 96.1 %all-gather.3.cloned.1.call-start = ((), (), s32[]{:S(2)}) async-start(), calls=%async_computation.5 | async-start | bytes 5391360 | tf_op jit(solution)/shard_map/all_gather | solution.py:81
  15.9 5.3 collective-permute-start
  19.9 4.6 collective-permute-start.1
  24.6 5.3 collective-permute-start.2
  28.6 5.5 collective-permute-start.3
  157.3 10.7 %collective-permute-start.4 = (bf16[32,32,384]{2,1,0:T(8,128)(2,1)S(1)}, bf16[32,32,384]{2,1,0:T(8,128)(2,1)S(1)}, u32[]{:S(2)}, u32[]{:S(2)}) collective-permute-start(bf16[32,32,384]{2,1,0:T(8,128)(2,1)S(1)} %broadcast_select_fusion), channel_id=1, source_target_pairs={{0,256},{1,257},{2,258},{3,259},{4,260},{5,261},{6,262},{7,263},{8... | collective-permute-start | bytes 2359304 | tf_op jit(solution)/shard_map/ppermute | solution.py:25
  172.6 2.7 collective-permute-start.5
  174.0 4.6 collective-permute-start.6
  178.7 3.5 collective-permute-start.7
  180.9 4.9 collective-permute-start.8
  186.3 2.8 slice-start
  187.4 1.7 slice-start.1
  217.8 5.0 copy-start.3
  219.0 22.6 %all-to-all-start.3 = ((bf16[8,4,8,4,384]{4,3,1,0,2:T(4,128)(2,1)}), bf16[8,4,8,4,384]{4,3,1,0,2:T(4,128)(2,1)S(1)}, u32[]{:S(2)}, u32[]{:S(2)}) async-start(bf16[8,4,8,4,384]{4,3,1,0,2:T(4,128)(2,1)} %copy.58), calls=%async_computation.3 | async-start | bytes 1572864 | tf_op jit(solution)/shard_map/all_to_all | solution.py:96
  222.5 719.8 %all-reduce.4.cloned.1.call-start = ((), (), s32[]{:S(2)}) async-start(), calls=%async_computation.4 | async-start | bytes 786432 | tf_op jit(solution)/shard_map/psum | solution.py:133
  243.0 1.1 copy-start.2
  244.1 1.2 copy-start.1
  244.1 1.2 copy-start.4
  824.8 123.2 %collective-permute-start.10 = (bf16[]{:T(256)}, bf16[]{:T(256)}, u32[]{:S(2)}, u32[]{:S(2)}) collective-permute-start(bf16[]{:T(256)} %convert_element_type.60), channel_id=1, source_target_pairs={{256,0},{257,1},{258,2},{259,3},{260,4},{261,5},{262,6},{263,7},{2... | collective-permute-start | bytes 14 | tf_op jit(solution)/shard_map/ppermute | solution.py:25
  945.7 2.9 collective-permute-start.9
Sparse Core Ops, SparseCore 0:
  11.7 91.6 all-gather.2
  247.5 225.9 all-reduce.3
where the time goes:
time: 958 us; the launch traced here: 957 us
  blocking collectives  643 us (67%)
  starting transfers between devices  141 us (15%)
  waiting for transfers between devices  97.9 us (10%)
  local copies, waits for them, and re-layouts  24 us (3%)
  between operations  18.2 us (2%)
  other arithmetic  17.5 us (2%)
  matrix products  16.1 us (2%)
    psum x1, blocking collectives, per_device(): gradient, loss_all = lax.psum((grad_total, loss_total), ('sy', 'sx', 'mb'))  575 us
    ppermute x3, starting transfers between devices, from_behind(): return lax.ppermute(block, axis, route)  120 us
    all_gather x1, waiting for transfers between devices, per_device(): lax.all_gather(conv_weight[0, 0], ('sy', 'sx'), axis=0, tiled=True)  57.8 us
    all_to_all x2, blocking collectives, per_device(): lax.all_to_all(outgoing, 'sy', split_axis=0, concat_axis=0, tiled=True)  47.8 us
    all_to_all x1, blocking collectives, per_device(): lax.all_to_all(lax.all_to_all(outgoing, 'sy', split_axis=0, concat_axis=0...  19.7 us
  transfers between devices with their start and end apart: 14, of which 7 were waited for; matrix products, arithmetic and copies ran while one was open for 3% of the time, Pallas kernels for 0%

commit v1 on v0

--- a/solution.py
+++ b/solution.py
@@ -130,7 +130,7 @@
         if tick_index < micro_count:
             handed = from_behind(moved, "section", 1)
     stacked = jnp.stack([jnp.where(first_section, first_out[0], second_out[0])])[None]
-    gradient, loss_all = lax.psum((grad_total, loss_total), ("sy", "sx", "mb"))
+    gradient, loss_all = lax.psum(lax.psum((grad_total, loss_total), "sy"), ("sx", "mb"))
     head_full = gradient * lax.rsqrt(jnp.mean(gradient * gradient) + 1e-06)
     mean_local = loss_all / (micro_count * lax.axis_size("mb") * cell_count * parts_y * parts_x)
     half_rows = channels // 2

time: 958 us -> 500 us (0.52)
  blocking collectives: 643 us -> 143 us
  waiting for transfers between devices: 97.9 us -> 224 us
  starting transfers between devices: 141 us -> 55.1 us
    psum x1 -> x2, blocking collectives: 575 us -> 75.4 us  [the longest x1 62.2 us: per_device(): lax.psum(lax.psum((grad_total, loss_total), 'sy'), ('sx', 'mb'))]
    psum x1 -> x2, waiting for transfers between devices: 0.01 us -> 128 us  [the longest x1 71.4 us: per_device(): lax.psum((grad_total, loss_total), 'sy')]
    ppermute x3, starting transfers between devices: 120 us -> 34.4 us  [from_behind(): return lax.ppermute(block, axis, route)]
  transfers between devices with their start and end apart: 14 -> 15, of which waited for: 7 -> 9; matrix products, arithmetic and copies ran while one was open for 3% -> 5% of each run, Pallas kernels for 0% -> 0%
where the time goes in v1:
time: 500 us; the launch traced here: 499 us
  waiting for transfers between devices  224 us (45%)
  blocking collectives  143 us (29%)
  starting transfers between devices  55.1 us (11%)
  local copies, waits for them, and re-layouts  24.6 us (5%)
  other arithmetic  18.4 us (4%)
  between operations  18 us (4%)
  matrix products  16 us (3%)
    psum x1, waiting for transfers between devices, per_device(): lax.psum((grad_total, loss_total), 'sy')  71.4 us
    psum x1, blocking collectives, per_device(): lax.psum(lax.psum((grad_total, loss_total), 'sy'), ('sx', 'mb'))  62.2 us
    all_gather x1, waiting for transfers between devices, per_device(): lax.all_gather(conv_weight[0, 0], ('sy', 'sx'), axis=0, tiled=True)  57.8 us
    psum x1, waiting for transfers between devices, per_device(): lax.psum(lax.psum((grad_total, loss_total), 'sy'), ('sx', 'mb'))  56.3 us
    all_to_all x2, blocking collectives, per_device(): lax.all_to_all(outgoing, 'sy', split_axis=0, concat_axis=0, tiled=True)  47.8 us
    ppermute x3, starting transfers between devices, from_behind(): return lax.ppermute(block, axis, route)  34.4 us
    all_to_all x1, blocking collectives, per_device(): lax.all_to_all(lax.all_to_all(outgoing, 'sy', split_axis=0, concat_axis=0...  19.7 us
    all_to_all x1, waiting for transfers between devices, per_device(): lax.all_to_all(lax.all_to_all(outgoing, 'sy', split_axis=0, concat_axis=0...  15 us
  transfers between devices with their start and end apart: 15, of which 9 were waited for; matrix products, arithmetic and copies ran while one was open for 5% of the time, Pallas kernels for 0%

profile of v1, /device:TPU:1, one launch (start us, length us, event | category | flops | bytes accessed | tf_op | source)
XLA Modules:
  0.0 499.0 jit_solution(12483775749994646203)
XLA Ops:
  12.0 3.8 fusion.20
  15.8 4.0 collective-permute-start
  21.2 3.3 collective-permute-done.1
  24.5 4.0 collective-permute-start.2
  29.9 4.2 collective-permute-done.3
  45.5 57.8 %all-gather.3.cloned.1.call-done = bf16[1,1,3456,384]{3,1,0,2:T(2,128)(2,1)} async-done(((bf16[1,1,54,384]{3,1,0,2:T(2,128)(2,1)}), bf16[1,1,3456,384]{3,1,0,2:T(2,128)(2,1)}) %all-gather.3.cloned.1.call-update) | async-done | bytes 2654224 | tf_op jit(solution)/shard_map/all_gather | solution.py:81
  103.3 8.4 %fusion.22 = bf16[32,32,384]{2,1,0:T(8,128)(2,1)S(1)} fusion(bf16[32,32,384]{2,1,0:T(8,128)(2,1)S(1)} %get-tuple-element.14, bf16[32,32,3456]{2,1,0:T(8,128)(2,1)} %slice_dynamic-update-slice_fusion.9, bf16[1,1,3456,384]{3,1,0,2:T(2,128)(2,1)} %all-gather.3.cloned.1.call-done), kind=kOutput, calls=%fused_computation.30 | convolution fusion | flops 2719088640 | bytes 11304960 | tf_op jit(solution)/shard_map/dot_general | solution.py:79
  112.3 23.7 %all_to_all.20 = bf16[8,4,8,4,384]{4,3,1,2,0:T(4,128)(2,1)S(1)} all-to-all(bf16[8,4,8,4,384]{4,3,1,2,0:T(4,128)(2,1)S(1)} %bitcast_select_fusion.2), channel_id=1, replica_groups=mesh['section'=2,'sy'=8,'sx'=8,'mb'=4] {'sy'}, dimensions={0} | all-to-all | bytes 1572864 | tf_op jit(solution)/shard_map/all_to_all | solution.py:97
  136.3 19.7 %all_to_all.21 = bf16[8,4,8,4,384]{4,3,1,0,2:T(4,128)(2,1)S(1)} all-to-all(bf16[8,4,8,4,384]{4,3,1,0,2:T(4,128)(2,1)S(1)} %copy.53), channel_id=1, replica_groups=mesh['section'=2,'sy'=8,'sx'=8,'mb'=4] {'sx'}, dimensions={2} | all-to-all | bytes 1572864 | tf_op jit(solution)/shard_map/all_to_all | solution.py:96
  158.8 9.2 %collective-permute-done.4 = bf16[32,32,384]{2,1,0:T(8,128)(2,1)S(1)} collective-permute-done((bf16[32,32,384]{2,1,0:T(8,128)(2,1)S(1)}, bf16[32,32,384]{2,1,0:T(8,128)(2,1)S(1)}, u32[]{:S(2)}, u32[]{:S(2)}) %collective-permute-start.4) | collective-permute-done | bytes 786464 | tf_op jit(solution)/shard_map/ppermute | solution.py:25
  168.7 3.8 fusion.13
  175.3 3.3 collective-permute-done.6
  182.1 3.6 collective-permute-done.8
  189.1 3.9 fusion.24
  193.6 24.2 %all_to_all.22 = bf16[8,4,8,4,384]{4,3,1,2,0:T(4,128)(2,1)S(1)} all-to-all(bf16[8,4,8,4,384]{4,3,1,2,0:T(4,128)(2,1)S(1)} %bitcast_select_fusion.1), channel_id=1, replica_groups=mesh['section'=2,'sy'=8,'sx'=8,'mb'=4] {'sy'}, dimensions={0} | all-to-all | bytes 1572864 | tf_op jit(solution)/shard_map/all_to_all | solution.py:97
  218.9 3.5 all-to-all-start.3
  223.9 2.6 copy.63
  226.5 15.0 %all-to-all-done.3 = bf16[8,4,8,4,384]{4,3,1,0,2:T(4,128)(2,1)S(1)} async-done(((bf16[8,4,8,4,384]{4,3,1,0,2:T(4,128)(2,1)}), bf16[8,4,8,4,384]{4,3,1,0,2:T(4,128)(2,1)S(1)}, u32[]{:S(2)}, u32[]{:S(2)}) %all-to-all-start.3) | async-done | bytes 786464 | tf_op jit(solution)/shard_map/all_to_all | solution.py:96
  247.4 71.4 %all-reduce.5.cloned.1.call-done = f32[384,256]{1,0:T(8,128)} async-done(((f32[384,256]{1,0:T(8,128)}), f32[384,256]{1,0:T(8,128)}) %all-reduce.5.cloned.1.call-update) | async-done | bytes 393232 | tf_op jit(solution)/shard_map/psum | solution.py:133
  320.1 13.2 %psum.30 = f32[]{:T(128)} all-reduce(f32[]{:T(128)S(6)} %select_n.85), channel_id=1, replica_groups=mesh['section'=2,'sy'=8,'sx'=8,'mb'=4] {'sy'}, use_global_device_ids=true, to_apply=%region_11.12 | all-reduce | flops 1 | bytes 8 | tf_op jit(solution)/shard_map/psum | solution.py:133
  333.2 62.2 %psum.31 = f32[]{:T(128)} all-reduce(f32[]{:T(128)} %psum.30), channel_id=1, replica_groups=mesh['section'=2,'sy'=8,'sx'=8,'mb'=4] {'sx','mb'}, use_global_device_ids=true, to_apply=%region_12.13 | all-reduce | flops 1 | bytes 8 | tf_op jit(solution)/shard_map/psum | solution.py:133
  396.3 25.9 %collective-permute-start.10 = (bf16[]{:T(256)}, bf16[]{:T(256)}, u32[]{:S(2)}, u32[]{:S(2)}) collective-permute-start(bf16[]{:T(256)} %convert_element_type.60), channel_id=1, source_target_pairs={{256,0},{257,1},{258,2},{259,3},{260,4},{261,5},{262,6},{263,7},{2... | collective-permute-start | bytes 14 | tf_op jit(solution)/shard_map/ppermute | solution.py:25
  422.2 56.3 %all-reduce.7.cloned.1.call-done = f32[384,256]{1,0:T(8,128)} async-done(((f32[384,256]{1,0:T(8,128)}), f32[384,256]{1,0:T(8,128)}) %all-reduce.7.cloned.1.call-update) | async-done | bytes 393232 | tf_op jit(solution)/shard_map/psum | solution.py:133
  482.0 7.0 %collective-permute-start.9 = (bf16[192,256]{1,0:T(8,128)(2,1)S(1)}, bf16[192,256]{1,0:T(8,128)(2,1)S(1)}, u32[]{:S(2)}, u32[]{:S(2)}) collective-permute-start(bf16[192,256]{1,0:T(8,128)(2,1)S(1)} %slice.157), channel_id=1, source_target_pairs={{256,0},{257,1},{258,2},{259,3},{260,4},{261,5},{262,6},{263,7},{2... | collective-permute-start | bytes 294920 | tf_op jit(solution)/shard_map/ppermute | solution.py:25
  (96 shorter events, 47.2 us)
Async XLA Ops:
  7.2 2.3 copy-start
  7.2 96.1 %all-gather.3.cloned.1.call-start = ((), (), s32[]{:S(2)}) async-start(), calls=%async_computation.6 | async-start | bytes 5391360 | tf_op jit(solution)/shard_map/all_gather | solution.py:81
  15.8 5.3 %collective-permute-start = (bf16[1,32,384]{2,1,0:T(8,128)(2,1)S(1)}, bf16[1,32,384]{2,1,0:T(8,128)(2,1)S(1)}, u32[]{:S(2)}, u32[]{:S(2)}) collective-permute-start(bf16[1,32,384]{2,1,0:T(8,128)(2,1)S(1)} %get-tuple-element.11), channel_id=1, source_target_pairs={{0,32},{32,64},{64,96},{96,128},{128,160},{160,192},{192,224},{1,3... | collective-permute-start | bytes 73736 | tf_op jit(solution)/shard_map/ppermute | solution.py:14
  19.9 4.6 collective-permute-start.1
  24.5 5.3 %collective-permute-start.2 = (bf16[34,1,384]{2,1,0:T(2,128)(2,1)S(1)}, bf16[34,1,384]{2,1,0:T(2,128)(2,1)S(1)}, u32[]{:S(2)}, u32[]{:S(2)}) collective-permute-start(bf16[34,1,384]{2,1,0:T(2,128)(2,1)S(1)} %get-tuple-element.7), channel_id=1, source_target_pairs={{0,4},{4,8},{8,12},{12,16},{16,20},{20,24},{24,28},{1,5},{5,9},{9,... | collective-permute-start | bytes 78344 | tf_op jit(solution)/shard_map/ppermute | solution.py:14
  28.6 5.5 %collective-permute-start.3 = (bf16[34,1,384]{2,1,0:T(2,128)(2,1)S(1)}, bf16[34,1,384]{2,1,0:T(2,128)(2,1)S(1)}, u32[]{:S(2)}, u32[]{:S(2)}) collective-permute-start(bf16[34,1,384]{2,1,0:T(2,128)(2,1)S(1)} %get-tuple-element.8), channel_id=1, source_target_pairs={{4,0},{8,4},{12,8},{16,12},{20,16},{24,20},{28,24},{5,1},{9,5},{13... | collective-permute-start | bytes 78344 | tf_op jit(solution)/shard_map/ppermute | solution.py:17
  157.3 10.7 %collective-permute-start.4 = (bf16[32,32,384]{2,1,0:T(8,128)(2,1)S(1)}, bf16[32,32,384]{2,1,0:T(8,128)(2,1)S(1)}, u32[]{:S(2)}, u32[]{:S(2)}) collective-permute-start(bf16[32,32,384]{2,1,0:T(8,128)(2,1)S(1)} %broadcast_select_fusion), channel_id=1, source_target_pairs={{0,256},{1,257},{2,258},{3,259},{4,260},{5,261},{6,262},{7,263},{8... | collective-permute-start | bytes 2359304 | tf_op jit(solution)/shard_map/ppermute | solution.py:25
  172.6 2.7 collective-permute-start.5
  174.0 4.6 collective-permute-start.6
  178.6 3.5 collective-permute-start.7
  180.8 4.9 collective-permute-start.8
  186.3 2.8 slice-start
  187.3 1.7 slice-start.1
  217.7 5.0 %copy-start.3 = (bf16[1,32,32,256]{3,2,1,0:T(8,128)(2,1)S(1)}, bf16[1,32,32,256]{3,2,1,0:T(8,128)(2,1)}, u32[]{:S(2)}) copy-start(bf16[1,32,32,256]{3,2,1,0:T(8,128)(2,1)} %param.12) | copy-start | bytes 1572868
  218.9 22.6 %all-to-all-start.3 = ((bf16[8,4,8,4,384]{4,3,1,0,2:T(4,128)(2,1)}), bf16[8,4,8,4,384]{4,3,1,0,2:T(4,128)(2,1)S(1)}, u32[]{:S(2)}, u32[]{:S(2)}) async-start(bf16[8,4,8,4,384]{4,3,1,0,2:T(4,128)(2,1)} %copy.58), calls=%async_computation.3 | async-start | bytes 1572864 | tf_op jit(solution)/shard_map/all_to_all | solution.py:96
  222.5 4.0 copy-start.5
  222.5 96.3 %all-reduce.5.cloned.1.call-start = ((), (), s32[]{:S(2)}) async-start(), calls=%async_computation.4 | async-start | bytes 786432 | tf_op jit(solution)/shard_map/psum | solution.py:133
  242.9 1.1 copy-start.2
  244.0 1.2 copy-start.1
  244.0 1.2 copy-start.4
  247.4 231.2 %all-reduce.7.cloned.1.call-start = ((), (), s32[]{:S(2)}) async-start(), calls=%async_computation.5 | async-start | bytes 786432 | tf_op jit(solution)/shard_map/psum | solution.py:133
  396.3 93.7 %collective-permute-start.10 = (bf16[]{:T(256)}, bf16[]{:T(256)}, u32[]{:S(2)}, u32[]{:S(2)}) collective-permute-start(bf16[]{:T(256)} %convert_element_type.60), channel_id=1, source_target_pairs={{256,0},{257,1},{258,2},{259,3},{260,4},{261,5},{262,6},{263,7},{2... | collective-permute-start | bytes 14 | tf_op jit(solution)/shard_map/ppermute | solution.py:25
  482.0 8.7 %collective-permute-start.9 = (bf16[192,256]{1,0:T(8,128)(2,1)S(1)}, bf16[192,256]{1,0:T(8,128)(2,1)S(1)}, u32[]{:S(2)}, u32[]{:S(2)}) collective-permute-start(bf16[192,256]{1,0:T(8,128)(2,1)S(1)} %slice.157), channel_id=1, source_target_pairs={{256,0},{257,1},{258,2},{259,3},{260,4},{261,5},{262,6},{263,7},{2... | collective-permute-start | bytes 294920 | tf_op jit(solution)/shard_map/ppermute | solution.py:25
Sparse Core Ops, SparseCore 0:
  11.7 91.6 all-gather.2
  247.5 71.2 all-reduce.4
  322.6 155.9 all-reduce.6
